TPU v7x, 32 devices: a whole 2x2x4 slice. The times are simulated.
32 devices in a mesh: fer: 4 (over z), bos: 8 (over y, x, core).
Axes of the slice: x: 2, y: 2, z: 4, core: 2. Of those that a mesh axis runs over, the one named last changes fastest.
Arguments:
- green: bfloat16 [4, 32, 9, 64, 128], P(None, 'fer', None, 'bos'), may hold values from -6 to 6
- bos_weight: bfloat16 [64, 9, 64, 128], P('bos'), may hold values from -12 to 12
- vertex: float32 [32, 64], P('fer', 'bos'), may hold values from 0.25 to 1.75
- block_order: int32 [8], replicated, may hold values from 0 to 7, each once
- window_start: int32 [1], replicated, may hold values from 0 to 32
Outputs:
- sigma: float32 [64, 32, 9, 128], P('bos', 'fer')
Inputs may be any that keep to these rules, and one draw needn't show every extreme that they name: block_order holds every block number once.
All inputs are finite; a program needn't handle non-finite values.
Results may differ from a plain program's by a relative error of at most 0.0003.
Values may be sent and summed in bfloat16 or wider, within the bound.
No kernel may reach another device: no remote copies, remote signals or barrier semaphores. Data moves between devices by JAX's collectives and lax.ppermute only.
A program may use at most 128 MiB of HBM per device.

v0:
```python
import math

import jax
import jax.numpy as jnp
from jax import lax
from jax.sharding import PartitionSpec as P

HIGHEST = lax.Precision.HIGHEST


def trig_tables(length):
    index = jnp.arange(length, dtype=jnp.int32)
    phase = (index[:, None] * index[None, :] % length).astype(jnp.float32) * (
        2.0 * math.pi / length
    )
    return (jnp.cos(phase), jnp.sin(phase))


def row_matrix(length, forward):
    cosine, sine = trig_tables(length)
    if forward:
        upper = jnp.concatenate([cosine, -sine], axis=1)
        lower = jnp.concatenate([sine, cosine], axis=1)
        block = jnp.concatenate([upper, lower], axis=0)
    else:
        upper = jnp.concatenate([cosine, sine], axis=1)
        lower = jnp.concatenate([-sine, cosine], axis=1)
        block = jnp.concatenate([upper, lower], axis=0) / length
    turned = jnp.concatenate([block[:, length:], -block[:, :length]], axis=1)
    return jnp.concatenate([block, turned], axis=1)


def col_tables(length, forward):
    cosine, sine = trig_tables(length)
    if forward:
        return (cosine, sine)
    return (cosine / length, -sine / length)


def row_step(field, matrix):
    return jnp.einsum("...c,cd->...d", field, matrix, precision=HIGHEST)


def col_step(halves, cos_part, sin_part):
    width = halves.shape[-1] // 2
    first = jnp.einsum("ax,nmxc->nmac", cos_part, halves[..., :width], precision=HIGHEST)
    return first + jnp.einsum("ax,nmxc->nmac", sin_part, halves[..., width:], precision=HIGHEST)


def body(green, bos_weight, vertex, block_order, window_start):
    num_fer = lax.axis_size("fer")
    fer_index = lax.axis_index("fer")
    bos_index = lax.axis_index("bos")
    num_slot = green.shape[0]
    window_dev = green.shape[1]
    orbitals = int(round(math.sqrt(green.shape[2])))
    bos_dev = bos_weight.shape[0]
    rows_all = bos_weight.shape[2]
    half_width = bos_weight.shape[3] // 2
    block_id = lax.dynamic_index_in_dim(block_order, bos_index, 0, keepdims=False)
    offset = window_start[0] + block_id * bos_dev
    shift_blocks = offset // window_dev
    inner = offset % window_dev
    shift_bits = shift_blocks % num_fer
    forward_rows = row_matrix(half_width, True)
    inverse_rows = row_matrix(half_width, False)
    forward_cos, forward_sin = col_tables(rows_all, True)
    inverse_cos, inverse_sin = col_tables(rows_all, False)
    full_rows = lax.all_gather(green, "bos", axis=3, tiled=True)
    everyone = lax.all_gather(full_rows[None], "fer", axis=0, tiled=True)
    sources = [
        lax.dynamic_index_in_dim(
            everyone, (fer_index + shift_bits + extra) % num_fer, 0, keepdims=False
        )
        for extra in range(3)
    ]
    picked = []
    for extra in range(3):
        slot = (fer_index + shift_blocks + extra) // num_fer % num_slot
        picked.append(lax.dynamic_index_in_dim(sources[extra], slot, 0, keepdims=False))
    blocks = jnp.concatenate(picked, axis=0)
    halves = row_step(blocks.astype(jnp.float32), forward_rows)
    green_real = col_step(halves, forward_cos, forward_sin)
    weight_real = col_step(
        row_step(bos_weight.astype(jnp.float32), inverse_rows), inverse_cos, inverse_sin
    )
    total = jnp.zeros((window_dev, orbitals * orbitals, rows_all, 2 * half_width), jnp.float32)
    for column in range(bos_dev):
        part = lax.dynamic_slice_in_dim(green_real, inner + column, window_dev, 0)
        part = part.reshape(window_dev, orbitals, orbitals, 1, rows_all, 2 * half_width)
        factor = weight_real[column].reshape(1, 1, orbitals, orbitals, rows_all, 2 * half_width)
        green_re, green_im = (part[..., :half_width], part[..., half_width:])
        weight_re, weight_im = (factor[..., :half_width], factor[..., half_width:])
        real_part = jnp.sum(green_re * weight_re - green_im * weight_im, axis=2)
        imag_part = jnp.sum(green_re * weight_im + green_im * weight_re, axis=2)
        product = jnp.concatenate([real_part, imag_part], axis=-1)
        product = product.reshape(window_dev, orbitals * orbitals, rows_all, 2 * half_width)
        total = total + vertex[:, column][:, None, None, None] * product
    sigma_halves = row_step(-total, inverse_rows)
    width = sigma_halves.shape[-1] // 2
    first = jnp.einsum("ax,nmxc->anmc", inverse_cos, sigma_halves[..., :width], precision=HIGHEST)
    return lax.psum_scatter(
        first
        + jnp.einsum("ax,nmxc->anmc", inverse_sin, sigma_halves[..., width:], precision=HIGHEST),
        "bos",
        scatter_dimension=0,
        tiled=True,
    )


def solution(mesh):
    return jax.shard_map(
        body,
        mesh=mesh,
        in_specs=(
            P(None, "fer", None, "bos", None),
            P("bos", None, None, None),
            P("fer", "bos"),
            P(),
            P(),
        ),
        out_specs=P("bos", "fer", None, None),
        check_vma=False,
    )
```

profile of v0, /device:TPU:0, one launch (start us, length us, event | category | flops | bytes accessed | tf_op | source)
XLA Modules:
  0.0 530.8 jit_solution(1642064408178534183)
XLA Ops:
  7.3 44.3 %all-gather.4.cloned.1.call-done = bf16[4,8,9,64,128]{4,3,2,1,0:T(8,128)(2,1)} async-done(((bf16[4,8,9,8,128]{4,3,2,1,0:T(8,128)(2,1)}), bf16[4,8,9,64,128]{4,3,2,1,0:T(8,128)(2,1)}) %all-gather.4.cloned.1.call-update) | async-done | bytes 4718608 | tf_op jit(solution)/shard_map/all_gather | solution.py:69
  55.2 2.1 convolution_bitcast_fusion
  57.3 2.5 fusion.17
  59.7 2.5 add_bitcast_fusion
  65.2 1.0 slice_bitcast_fusion.25
  69.0 306.8 %all-gather.6.cloned.1.call-done = bf16[16,8,9,64,128]{4,3,2,1,0:T(8,128)(2,1)} async-done(((bf16[4,8,9,64,128]{4,3,2,1,0:T(8,128)(2,1)}), bf16[16,8,9,64,128]{4,3,2,1,0:T(8,128)(2,1)}) %all-gather.6.cloned.1.call-update) | async-done | bytes 18874384 | tf_op jit(solution)/shard_map/all_gather | solution.py:70
  375.8 2.8 dynamic-slice_bitcast_fusion.2
  378.6 6.1 %fusion.4 = f32[24,9,64,256]{3,2,1,0:T(8,128)S(1)} fusion(bf16[8,9,64,128]{3,2,1,0:T(8,128)(2,1)S(1)} %get-tuple-element.30, bf16[8,9,64,128]{3,2,1,0:T(8,128)(2,1)S(1)} %get-tuple-element.31, bf16[8,9,64,128]{3,2,1,0:T(8,128)(2,1)S(1)} %get-tuple-element.29, f32[128,64]{1,0:T(8,128)S(1)} %get-tuple-element.83, f32[128,64]{1,0:T(8,128)S(1)} %get-tuple-element.82, ...), kind=kOutput, calls=%fused_computation.20 | convolution fusion | flops 5439520768 | bytes 17809408 | tf_op jit(solution)/shard_map/...c,cd->...d/dot_general | solution.py:41
  384.7 5.0 copy-done.2
  389.7 7.3 %fusion = f32[24,9,128,64]{2,3,1,0:T(8,128)S(1)} fusion(f32[24,9,64,256]{3,2,1,0:T(8,128)S(1)} %fusion.4), kind=kOutput, calls=%fused_computation | convolution fusion | flops 1359011840 | bytes 14155776 | tf_op jit(solution)/shard_map/ax,nmxc->nmac/dot_general | solution.py:47
  397.1 9.7 %fusion.10 = f32[24,9,128,64]{2,3,1,0:T(8,128)S(1)} fusion(f32[24,9,128,64]{2,3,1,0:T(8,128)S(1)} %fusion, f32[24,9,64,256]{3,2,1,0:T(8,128)} %copy-done.2), kind=kOutput, calls=%fused_computation.26 | convolution fusion | flops 1360781312 | bytes 21233664 | tf_op jit(solution)/shard_map/ax,nmxc->nmac/dot_general | solution.py:46
  406.7 4.7 constant_dynamic-slice_fusion.7
  411.5 4.8 slice_bitcast_fusion.15
  416.2 2.5 slice_bitcast_fusion.13
  418.7 3.1 slice_bitcast_fusion.11
  421.9 3.1 slice_bitcast_fusion.9
  425.0 2.3 slice_bitcast_fusion.7
  430.7 3.5 subtract_reduce_fusion.7
  434.9 1.0 copy-done.11
  436.0 3.3 subtract_reduce_fusion.6
  441.7 3.3 subtract_reduce_fusion.5
  447.5 3.3 subtract_reduce_fusion.4
  451.5 1.0 copy-done.6
  452.6 3.5 subtract_reduce_fusion.3
  457.1 3.3 subtract_reduce_fusion.2
  461.4 3.3 subtract_reduce_fusion.1
  465.4 3.5 subtract_reduce_fusion
  469.8 4.8 fusion.21
  474.6 2.3 fusion.13
  476.9 3.8 fusion.40
  480.8 41.3 %reduce-scatter.2.cloned.1.call-done = f32[8,8,9,128]{3,0,2,1:T(8,128)} async-done(((f32[64,8,9,128]{3,0,2,1:T(8,128)}), f32[8,8,9,128]{3,0,2,1:T(8,128)}) %reduce-scatter.2.cloned.1.call-update) | async-done | bytes 294928 | tf_op jit(solution)/shard_map/reduce_scatter | solution.py:102
  522.1 1.7 copy.8
  (91 shorter events, 21.8 us)
Async XLA Ops:
  6.5 48.7 %copy-start = (bf16[8,9,64,128]{3,2,1,0:T(8,128)(2,1)S(1)}, bf16[8,9,64,128]{3,2,1,0:T(8,128)(2,1)}, u32[]{:S(2)}) copy-start(bf16[8,9,64,128]{3,2,1,0:T(8,128)(2,1)} %param.6) | copy-start | bytes 3538948
  6.5 45.1 %all-gather.4.cloned.1.call-start = ((), (), s32[]{:S(2)}) async-start(), calls=%async_computation.1 | async-start | bytes 5308416 | tf_op jit(solution)/shard_map/all_gather | solution.py:69
  7.3 368.5 %all-gather.6.cloned.1.call-start = ((), (), s32[]{:S(2)}) async-start(), calls=%async_computation.3 | async-start | bytes 23592960 | tf_op jit(solution)/shard_map/all_gather | solution.py:70
  51.6 2.3 copy-start.28
  51.6 470.5 %reduce-scatter.2.cloned.1.call-start = ((), (), s32[]{:S(2)}) async-start(), calls=%async_computation.2 | async-start | bytes 2654208 | tf_op jit(solution)/shard_map/reduce_scatter | solution.py:102
  55.2 2.1 copy-start.26
  384.7 5.1 copy-start.2
  411.5 4.8 copy-start.5
  416.2 2.5 copy-start.4
  418.7 3.2 copy-start.3
  429.0 1.7 copy-start.12
  429.0 1.7 copy-start.24
  429.0 1.7 copy-start.25
  434.2 1.7 copy-start.11
  434.2 1.7 copy-start.22
  434.2 1.7 copy-start.23
  439.3 1.7 copy-start.9
  439.3 2.4 copy-start.10
  439.3 2.4 copy-start.20
  439.3 2.4 copy-start.21
  445.0 1.7 copy-start.7
  445.0 2.4 copy-start.8
  445.1 2.4 copy-start.18
  445.1 2.4 copy-start.19
  450.8 1.7 copy-start.6
  450.8 1.7 copy-start.16
  450.8 1.7 copy-start.17
  456.1 1.0 copy-start.14
  456.1 1.0 copy-start.15
  460.4 1.0 copy-start.13
  468.9 0.8 copy-start.27
  476.9 47.0 %copy-start.1 = (bf16[8,9,64,128]{3,2,1,0:T(8,128)(2,1)S(1)}, bf16[8,9,64,128]{3,2,1,0:T(8,128)(2,1)}, u32[]{:S(2)}) copy-start(bf16[8,9,64,128]{3,2,1,0:T(8,128)(2,1)} %param.6) | copy-start | bytes 3538948
  (2 other events, 1.6 us)
Sparse Core Ops, SparseCore 0:
  9.2 42.3 all-gather.3
  53.2 322.5 all-gather.5
  480.9 41.1 reduce-scatter.1
where the time goes:
time: 540 us; the launch traced here: 531 us
  waiting for transfers between devices  393 us (73%)
  local copies, waits for them, and re-layouts  48 us (9%)
  matrix products  41 us (8%)
  other arithmetic  32.9 us (6%)
  between operations  15.6 us (3%)
    all_gather x1, waiting for transfers between devices, body(): everyone = lax.all_gather(full_rows[None], 'fer', axis=0, tiled=True)  307 us
    all_gather x1, waiting for transfers between devices, body(): full_rows = lax.all_gather(green, 'bos', axis=3, tiled=True)  44.3 us
    reduce_scatter x1, waiting for transfers between devices, body(): lax.psum_scatter(first + jnp.einsum('ax,nmxc->anmc', inverse_sin, sigma_h...  41.3 us
    reduce_sum x8, other arithmetic, body(): real_part = jnp.sum(green_re * weight_re - green_im * weight_im, axis=2)  27 us
    mul x16, local copies, waits for them, and re-layouts, body(): real_part = jnp.sum(green_re * weight_re - green_im * weight_im, axis=2)  24.8 us
    dot_general x3, matrix products, row_step(): return jnp.einsum('...c,cd->...d', field, matrix, precision=HIGHEST)  12.9 us
    unnamed x62, local copies, waits for them, and re-layouts  12.4 us
    dot_general x2, matrix products, col_step(): jnp.einsum('ax,nmxc->nmac', cos_part, halves[..., :width], precision=HIGH...  12.1 us
  transfers between devices with their start and end apart: 3, of which 3 were waited for; matrix products, arithmetic and copies ran while one was open for 3% of the time, Pallas kernels for 0%

commit v1 on v0

--- a/solution.py
+++ b/solution.py
@@ -1,11 +1,17 @@
+import functools
 import math
 
 import jax
 import jax.numpy as jnp
+import numpy as np
 from jax import lax
+from jax.experimental import pallas as pl
+from jax.experimental.pallas import tpu as pltpu
 from jax.sharding import PartitionSpec as P
 
 HIGHEST = lax.Precision.HIGHEST
+SUBLANES = 8
+LANES = 128
 
 
 def trig_tables(length):
@@ -47,7 +53,7 @@
     return first + jnp.einsum("ax,nmxc->nmac", sin_part, halves[..., width:], precision=HIGHEST)
 
 
-def body(green, bos_weight, vertex, block_order, window_start):
+def gathered_body(green, bos_weight, vertex, block_order, window_start):
     num_fer = lax.axis_size("fer")
     fer_index = lax.axis_index("fer")
     bos_index = lax.axis_index("bos")
@@ -108,6 +114,256 @@
     )
 
 
+def turn(out_index, in_index, length, sign):
+    phase = 2.0 * np.pi * (np.multiply.outer(out_index, in_index) % length) / length
+    cosine, sine = np.cos(phase), sign * np.sin(phase)
+    return np.stack([np.stack([cosine, -sine]), np.stack([sine, cosine])])
+
+
+@functools.lru_cache(None)
+def tables(num_fer, num_bos, rows_all, cols):
+    devices = num_fer * num_bos
+    near = cols // devices
+    kx_dev = rows_all // num_bos
+    ry, ky = np.arange(cols), np.arange(cols)
+    rx, kx = np.arange(rows_all), np.arange(rows_all)
+    eye = np.eye(near)
+    t = turn(ry, ky, cols, -1.0)
+    to_ry = t.transpose(2, 0, 1, 3).reshape(2 * cols, 2 * cols)
+    t = turn(rx, kx, rows_all, -1.0).reshape(2, 2, rows_all, num_bos, kx_dev)
+    to_rx = np.einsum("oirbk,nm->bnikomr", t, eye).reshape(
+        2 * near * rows_all, 2 * near * rows_all
+    )
+    t = turn(kx, rx, rows_all, 1.0).reshape(2, 2, num_bos, kx_dev, rows_all)
+    to_kx = -np.einsum("oibkr,nm->bnokimr", t, eye).reshape(
+        2 * near * rows_all, 2 * near * rows_all
+    ) / rows_all
+    t = turn(ky, ry, cols, 1.0) / cols
+    to_ky = t.transpose(3, 1, 0, 2).reshape(2 * cols, 2 * cols)
+    t = turn(ry, ky, cols, 1.0).reshape(2, 2, num_fer, num_bos, near, cols) / cols
+    weight_ry = t.transpose(2, 1, 5, 3, 4, 0).reshape(num_fer, 2 * cols, num_bos * near * 2)
+    weight_rx = turn(rx, kx, rows_all, 1.0).transpose(3, 1, 0, 2) / rows_all
+    out = (to_ry, to_rx, to_kx, to_ky, weight_ry, weight_rx)
+    return tuple(np.ascontiguousarray(x, dtype=np.float32) for x in out)
+
+
+def nt_dot(a, b):
+    return lax.dot_general(
+        a, b, (((1,), (1,)), ((), ())), precision=HIGHEST, preferred_element_type=jnp.float32
+    )
+
+
+def nn_dot(a, b):
+    return lax.dot_general(
+        a, b, (((1,), (0,)), ((), ())), precision=HIGHEST, preferred_element_type=jnp.float32
+    )
+
+
+def send_green_kernel(devices, spans, window, start_ref, green_ref, vertex_ref, table_ref, out_ref, rows_ref, part_ref):
+    num_slot, held, pairs, kx_dev, width = green_ref.shape
+    used = spans * pairs * held
+    start = start_ref[0]
+    first_slot = start // window
+    spill = start % window - lax.axis_index("fer") * held
+    for span in range(spans):
+        for u in range(held):
+            slot = jnp.minimum(first_slot + span + (u < spill).astype(jnp.int32), num_slot - 1)
+            block = green_ref[slot, u].astype(jnp.float32)
+            base = (span * held + u) * pairs * kx_dev
+            rows_ref[pl.ds(base, pairs * kx_dev), :] = block.reshape(pairs * kx_dev, width)
+    part_ref[pl.ds(used, part_ref.shape[0] - used), :] = jnp.zeros(
+        (part_ref.shape[0] - used, width), jnp.float32
+    )
+    halves = part_ref.shape[0] // LANES
+    blocks = out_ref.shape[0] // (halves * kx_dev)
+    for kx in range(kx_dev):
+        for span in range(spans):
+            for pair in range(pairs):
+                base = (span * held * pairs + pair) * kx_dev + kx
+                part_ref[pl.ds((span * pairs + pair) * held, held), :] = rows_ref[
+                    pl.ds(base, held, stride=pairs * kx_dev), :
+                ]
+        moved = nt_dot(table_ref[...], part_ref[...])
+        for half in range(halves):
+            out_ref[pl.ds(half * kx_dev + kx, blocks, stride=halves * kx_dev), :] = moved[
+                :, half * LANES : (half + 1) * LANES
+            ]
+    tile = vertex_ref[...]
+    at = used - (halves - 1) * LANES
+    for dest in range(devices):
+        row = (dest * blocks // devices * halves + halves - 1) * kx_dev
+        out_ref[pl.ds(row, held), at : at + tile.shape[1]] = tile
+
+
+def convolve_kernel(
+    num_fer, num_bos, spans, window, start_ref, order_ref, green_ref, weight_ref, to_rx_ref, to_kx_ref,
+    out_ref, planes_ref, factor_ref, scale_ref,
+):
+    held = window // num_fer
+    pairs = 9
+    bos_dev = weight_ref.shape[0] // (num_bos * 2 * pairs)
+    used = spans * pairs * held
+    points = LANES
+    quads, halves, kx_dev, _ = green_ref.shape
+    quads = quads // num_fer
+    depth = quads * kx_dev
+    start = start_ref[0]
+    turn_by = lax.rem(window - start % window, window)
+    moved = []
+    for fer in range(num_fer):
+        turned = []
+        for half in range(halves):
+            block = green_ref[pl.ds(fer * quads, quads), half].reshape(depth, LANES)
+            turned.append(block.T)
+        moved.append(nn_dot(jnp.concatenate(turned, axis=0)[:used], to_rx_ref[...]))
+    for span in range(spans):
+        for pair in range(pairs):
+            row = (span * pairs + pair) * held
+            both = []
+            for part in range(2):
+                group = jnp.concatenate(
+                    [m[row : row + held, part * points : (part + 1) * points] for m in moved], axis=0
+                )
+                both.append(pltpu.roll(group, turn_by, 0))
+            where = pl.ds(span * window, window)
+            planes_ref[pair, where, :] = both[0] + both[1]
+            planes_ref[pairs + pair, where, :] = both[0]
+            planes_ref[2 * pairs + pair, where, :] = both[1]
+    for cb in range(pairs):
+        re = weight_ref[pl.ds(2 * cb, num_bos * bos_dev, stride=2 * pairs), :]
+        im = weight_ref[pl.ds(2 * cb + 1, num_bos * bos_dev, stride=2 * pairs), :]
+        factor_ref[cb] = re
+        factor_ref[pairs + cb] = im - re
+        factor_ref[2 * pairs + cb] = re + im
+    at = used - (halves - 1) * LANES
+    for fer in range(num_fer):
+        for bos in range(num_bos):
+            tile = green_ref[(fer * num_bos + bos) * quads // num_bos, halves - 1, :, at : at + bos_dev]
+            for column in range(bos_dev):
+                scale_ref[(fer * num_bos + bos) * bos_dev + column] = jnp.broadcast_to(
+                    tile[:, column : column + 1], (held, points)
+                )
+    orbitals = 3
+    for fer in range(num_fer):
+
+        def step(p, sums):
+            omega = order_ref[p // bos_dev] * bos_dev + p % bos_dev
+            where = pl.ds(fer * held + omega, held)
+            scale = scale_ref[fer * num_bos * bos_dev + p]
+            sums = list(sums)
+            for third in range(3):
+                g = [planes_ref[third * pairs + pair, where, :] for pair in range(pairs)]
+                f = [factor_ref[third * pairs + cb, pl.ds(p, 1), :] * scale for cb in range(pairs)]
+                for a in range(orbitals):
+                    for b in range(orbitals):
+                        value = g[a * orbitals] * f[b]
+                        for c in range(1, orbitals):
+                            value = value + g[a * orbitals + c] * f[c * orbitals + b]
+                        at = third * pairs + a * orbitals + b
+                        sums[at] = sums[at] + value
+            return tuple(sums)
+
+        zero = jnp.zeros((held, points), jnp.float32)
+        sums = lax.fori_loop(0, num_bos * bos_dev, step, (zero,) * (3 * pairs))
+        re = jnp.concatenate([sums[i] - sums[2 * pairs + i] for i in range(pairs)], axis=0)
+        im = jnp.concatenate([sums[i] + sums[pairs + i] for i in range(pairs)], axis=0)
+        sigma = jnp.concatenate([re, im], axis=1)
+        out_ref[pl.ds(fer * depth, depth), : pairs * held] = nt_dot(to_kx_ref[...], sigma)
+
+
+def finish_kernel(held, sum_ref, table_ref, out_ref):
+    kx_dev, rows, width = out_ref.shape
+    pairs = rows // held
+    deep = sum_ref.shape[0] // kx_dev
+    for kx in range(kx_dev):
+        block = sum_ref[pl.ds(kx, deep, stride=kx_dev), :]
+        done = nn_dot(block.T[:rows], table_ref[...])
+        for pair in range(pairs):
+            out_ref[kx, pl.ds(pair, held, stride=pairs), :] = done[pair * held : (pair + 1) * held]
+
+
+def real_space_body(green, bos_weight, vertex, block_order, window_start):
+    num_fer, num_bos = lax.axis_size("fer"), lax.axis_size("bos")
+    devices = num_fer * num_bos
+    num_slot, held, pairs, kx_dev, width = green.shape
+    bos_dev, _, rows_all, _ = bos_weight.shape
+    cols = width // 2
+    near = cols // devices
+    window = held * num_fer
+    spans = -(-(window + num_bos * bos_dev) // window)
+    to_ry, to_rx, to_kx, to_ky, weight_ry, weight_rx = tables(num_fer, num_bos, rows_all, cols)
+    vmem = pl.BlockSpec(memory_space=pltpu.VMEM)
+    smem = pl.BlockSpec(memory_space=pltpu.SMEM)
+    lanes = 2 * LANES
+    message = pl.pallas_call(
+        functools.partial(send_green_kernel, devices, spans, window),
+        out_shape=jax.ShapeDtypeStruct((devices * 2 * near * 2 * kx_dev, LANES), jnp.float32),
+        in_specs=[smem, vmem, vmem, vmem],
+        out_specs=vmem,
+        scratch_shapes=[
+            pltpu.VMEM((spans * held * pairs * kx_dev, width), jnp.float32),
+            pltpu.VMEM((lanes, width), jnp.float32),
+        ],
+        name="send_green",
+    )(window_start, green, vertex, to_ry)
+    mine = lax.dynamic_index_in_dim(weight_ry, lax.axis_index("fer"), 0, keepdims=False)
+    part = jnp.einsum("pmkc,cd->pmkd", bos_weight.astype(jnp.float32), mine, precision=HIGHEST)
+    part = part.reshape(bos_dev, pairs, rows_all, num_bos, near, 2)
+    factors = jnp.einsum("pmkbni,kior->bpmonr", part, weight_rx, precision=HIGHEST)
+    factors = factors.reshape(num_bos, bos_dev * pairs * 2, near * rows_all)
+    factors = lax.all_to_all(factors, "bos", 0, 0, tiled=True)
+    message = message.reshape(devices, 2 * near * 2 * kx_dev, LANES)
+    message = lax.all_to_all(message, ("fer", "bos"), 0, 0, tiled=True)
+    total_rows = devices * 2 * near * kx_dev
+    sums = pl.pallas_call(
+        functools.partial(convolve_kernel, num_fer, num_bos, spans, window),
+        out_shape=jax.ShapeDtypeStruct((total_rows, LANES), jnp.float32),
+        in_specs=[smem, smem, vmem, vmem, vmem, vmem],
+        out_specs=vmem,
+        scratch_shapes=[
+            pltpu.VMEM((3 * pairs, spans * window, LANES), jnp.float32),
+            pltpu.VMEM((3 * pairs, num_bos * bos_dev, LANES), jnp.float32),
+            pltpu.VMEM((num_fer * num_bos * bos_dev, held, LANES), jnp.float32),
+        ],
+        name="convolve",
+    )(
+        window_start,
+        block_order,
+        message.reshape(devices * 2 * near, 2, kx_dev, LANES),
+        factors.reshape(num_bos * bos_dev * pairs * 2, LANES),
+        to_rx,
+        to_kx,
+    )
+    sums = lax.all_to_all(
+        sums.reshape(devices, 2 * near * kx_dev, LANES), ("fer", "bos"), 0, 0, tiled=True
+    )
+    out = pl.pallas_call(
+        functools.partial(finish_kernel, held),
+        out_shape=jax.ShapeDtypeStruct((kx_dev, held * pairs, width), jnp.float32),
+        in_specs=[vmem, vmem],
+        out_specs=vmem,
+        name="finish",
+    )(sums.reshape(total_rows, LANES), to_ky)
+    return out.reshape(kx_dev, held, pairs, width)
+
+
+def body(green, bos_weight, vertex, block_order, window_start):
+    devices = lax.axis_size("fer") * lax.axis_size("bos")
+    num_slot, held, pairs, kx_dev, width = green.shape
+    bos_dev, _, rows_all, _ = bos_weight.shape
+    cols = width // 2
+    fits = (
+        devices == 32
+        and cols % devices == 0
+        and (cols // devices) * rows_all == LANES
+        and width == LANES
+        and pairs == 9
+        and held == kx_dev == bos_dev == SUBLANES
+    )
+    plan = real_space_body if fits else gathered_body
+    return plan(green, bos_weight, vertex, block_order, window_start)
+
+
 def solution(mesh):
     return jax.shard_map(
         body,

time: 540 us -> 96.9 us (0.18); the launches traced: 531 us -> 96.4 us
  waiting for transfers between devices: 393 us -> 5.6 us
  blocking collectives: 0 us -> 49.6 us
  local copies, waits for them, and re-layouts: 48 us -> 5.64 us
  matrix products: 41 us -> 6.24 us
  other arithmetic: 32.9 us -> 0 us
  Pallas kernels: 0 us -> 23.3 us
  between operations: 15.6 us -> 0.7 us
    all_gather x2 -> x0, waiting for transfers between devices: 351 us -> none  [the longest x1 307 us: body(): everyone = lax.all_gather(full_rows[None], 'fer', axis=0, tiled=True)]
    all_to_all x0 -> x2, blocking collectives: none -> 49.6 us  [the longest x1 30.3 us: real_space_body(): message = lax.all_to_all(message, ('fer', 'bos'), 0, 0, tiled=True)]
    reduce_scatter x1 -> x0, waiting for transfers between devices: 41.3 us -> none  [body(): lax.psum_scatter(first + jnp.einsum('ax,nmxc->anmc', inverse_sin, sigma_h...]
    dot_general x9 -> x2, matrix products: 41 us -> 6.24 us  [the longest x1 4.04 us: real_space_body(): jnp.einsum('pmkc,cd->pmkd', bos_weight.astype(jnp.float32), mine, precisi...]
    reduce_sum x8 -> x0, other arithmetic: 27 us -> none  [body(): real_part = jnp.sum(green_re * weight_re - green_im * weight_im, axis=2)]
    mul x16 -> x0, local copies, waits for them, and re-layouts: 24.8 us -> none  [body(): real_part = jnp.sum(green_re * weight_re - green_im * weight_im, axis=2)]
    pallas_call x0 -> x3, Pallas kernels: none -> 23.3 us  [the longest x1 16.7 us: real_space_body(): pl.pallas_call(functools.partial(convolve_kernel, num_fer, num_bos, spans...]
    unnamed x62 -> x6, local copies, waits for them, and re-layouts: 12.4 us -> 1.28 us
  transfers between devices with their start and end apart: 3 -> 1, of which waited for: 3 -> 1; matrix products, arithmetic and copies ran while one was open for 3% -> 0% of each run, Pallas kernels for 0% -> 4%
where the time goes in v1:
time: 96.9 us; the launch traced here: 96.4 us
  blocking collectives  49.6 us (51%)
  Pallas kernels  23.3 us (24%)
  matrix products  6.24 us (6%)
  local copies, waits for them, and re-layouts  5.64 us (6%)
  waiting for transfers between devices  5.6 us (6%)
  starting transfers between devices  5.2 us (5%)
    all_to_all x1, blocking collectives, real_space_body(): message = lax.all_to_all(message, ('fer', 'bos'), 0, 0, tiled=True)  30.3 us
    all_to_all x1, blocking collectives, real_space_body(): lax.all_to_all(sums.reshape(devices, 2 * near * kx_dev, LANES), ('fer', '...  19.3 us
    pallas_call x1, Pallas kernels, real_space_body(): pl.pallas_call(functools.partial(convolve_kernel, num_fer, num_bos, spans...  16.7 us
    all_to_all x1, waiting for transfers between devices, real_space_body(): factors = lax.all_to_all(factors, 'bos', 0, 0, tiled=True)  5.6 us
    all_to_all x1, starting transfers between devices, real_space_body(): factors = lax.all_to_all(factors, 'bos', 0, 0, tiled=True)  5.2 us
    pallas_call x1, Pallas kernels, real_space_body(): pl.pallas_call(functools.partial(send_green_kernel, devices, spans, windo...  4.17 us
    dot_general x1, matrix products, real_space_body(): jnp.einsum('pmkc,cd->pmkd', bos_weight.astype(jnp.float32), mine, precisi...  4.04 us
    pallas_call x1, Pallas kernels, real_space_body(): pl.pallas_call(functools.partial(finish_kernel, held), out_shape=jax.Shap...  2.44 us
  transfers between devices with their start and end apart: 1, of which 1 were waited for; matrix products, arithmetic and copies ran while one was open for 0% of the time, Pallas kernels for 4%

profile of v1, /device:TPU:0, one launch (start us, length us, event | category | flops | bytes accessed | tf_op | source)
XLA Modules:
  0.0 96.4 jit_solution(17695680816713347211)
XLA Ops:
  0.0 0.0 copy-start
  0.0 1.3 %copy-done = bf16[8,9,64,128]{3,2,1,0:T(8,128)(2,1)S(1)} copy-done((bf16[8,9,64,128]{3,2,1,0:T(8,128)(2,1)S(1)}, bf16[8,9,64,128]{3,2,1,0:T(8,128)(2,1)}, u32[]{:S(2)}) %copy-start) | copy-done | bytes 1179672
  1.3 0.0 copy-start.2
  1.3 4.0 %fusion.5 = f32[32,8,9,64]{3,0,2,1:T(8,128)S(1)} fusion(bf16[8,9,64,128]{3,2,1,0:T(8,128)(2,1)S(1)} %copy-done, f32[4,128,32]{1,2,0:T(8,128)} %constant.24.clone, s32[]{:T(128)S(6)} %select_n.4), kind=kOutput, calls=%fused_computation.3 | convolution fusion | flops 226492416 | bytes 1785860 | tf_op jit(solution)/shard_map/pmkc,cd->pmkd/dot_general | solution.py:310
  5.3 0.0 copy-done.2
  5.3 2.2 %fusion.2 = f32[8,8,9,2,2,64]{5,2,3,4,0,1:T(8,128)S(1)} fusion(f32[64,2,2,64,1,1,1]{3,0,1,2,6,5,4:T(8,128)S(1)} %copy-done.2, f32[8,9,64,8,2,2,1]{2,5,4,3,1,0,6:T(2,128)S(1)} %bitcast.28), kind=kOutput, calls=%fused_computation.2 | convolution fusion | flops 226492416 | bytes 1245184 | tf_op jit(solution)/shard_map/pmkbni,kior->bpmonr/dot_general | solution.py:312
  7.5 1.1 %copy.15 = f32[8,8,9,2,2,64]{5,4,3,2,1,0:T(2,128)S(1)} copy(f32[8,8,9,2,2,64]{5,2,3,4,0,1:T(8,128)S(1)} %fusion.2) | data formatting | bytes 1179648 | tf_op jit(solution)/shard_map/pmkbni,kior->bpmonr/transpose | solution.py:312
  8.6 1.5 %reshape.27 = f32[8,144,128]{2,1,0:T(8,128)} reshape(f32[8,8,9,2,2,64]{5,4,3,2,1,0:T(2,128)S(1)} %copy.15) | data formatting | bytes 1179648 | tf_op jit(solution)/shard_map/reshape | solution.py:313
  10.1 5.2 %all-to-all-start.1 = ((f32[8,144,128]{2,1,0:T(8,128)}), f32[8,144,128]{2,1,0:T(8,128)S(1)}, u32[]{:S(2)}, u32[]{:S(2)}) async-start(f32[8,144,128]{2,1,0:T(8,128)} %reshape.27), calls=%async_computation.1 | async-start | bytes 1179648 | tf_op jit(solution)/shard_map/all_to_all | solution.py:314
  16.0 4.2 %send_green.1 = f32[2048,128]{1,0:T(8,128)} custom-call(s32[1]{0:T(128)S(6)} %copy.28.start_ref, bf16[4,8,9,8,128]{4,3,2,1,0:T(8,128)(2,1)} %green_ref.1, f32[8,8]{1,0:T(8,128)} %vertex_ref.1, f32[128,128]{1,0:T(8,128)} %constant.23.clone.table_ref), custom_call_target="tpu_custom_call" | custom-call | tf_op jit(solution)/shard_map/send_green/pallas_call | solution.py:298
  20.1 5.6 %all-to-all-done.1 = f32[8,144,128]{2,1,0:T(8,128)S(1)} async-done(((f32[8,144,128]{2,1,0:T(8,128)}), f32[8,144,128]{2,1,0:T(8,128)S(1)}, u32[]{:S(2)}, u32[]{:S(2)}) %all-to-all-start.1) | async-done | bytes 589856 | tf_op jit(solution)/shard_map/all_to_all | solution.py:314
  25.7 0.0 copy-start.1
  25.7 30.3 %all_to_all.15 = f32[32,64,128]{2,1,0:T(8,128)} all-to-all(f32[32,64,128]{2,1,0:T(8,128)} %bitcast.30), channel_id=1, replica_groups=mesh['fer'=4,'bos'=8] {'fer','bos'}, dimensions={0} | all-to-all | bytes 2097152 | tf_op jit(solution)/shard_map/all_to_all | solution.py:316
  56.0 0.0 copy-done.1
  56.0 16.7 %convolve.1 = f32[1024,128]{1,0:T(8,128)} custom-call(s32[1]{0:T(128)S(6)} %copy.28.start_ref, s32[8]{0:T(128)} %order_ref.1, f32[128,2,8,128]{3,2,1,0:T(8,128)} %bitcast.29, f32[1152,128]{1,0:T(8,128)} %bitcast.31, f32[256,256]{1,0:T(8,128)} %constant.26.clone.to_rx_ref, f32[256,256]{1,0:T(8,128)} %constant.27.clone.to_kx_ref), custom_call_target="tpu_custom_call" | custom-call | tf_op jit(solution)/shard_map/convolve/pallas_call | solution.py:318
  72.8 19.3 %all_to_all.16 = f32[32,32,128]{2,1,0:T(8,128)} all-to-all(f32[32,32,128]{2,1,0:T(8,128)} %bitcast.32), channel_id=1, replica_groups=mesh['fer'=4,'bos'=8] {'fer','bos'}, dimensions={0} | all-to-all | bytes 1048576 | tf_op jit(solution)/shard_map/all_to_all | solution.py:337
  92.1 2.4 %finish.1 = f32[8,72,128]{2,1,0:T(8,128)} custom-call(f32[1024,128]{1,0:T(8,128)} %bitcast.33, f32[128,128]{1,0:T(8,128)} %constant.28.clone.table_ref), custom_call_target="tpu_custom_call" | custom-call | tf_op jit(solution)/shard_map/finish/pallas_call | solution.py:340
  94.6 1.0 %copy.16 = f32[8,72,128]{2,0,1:T(8,128)S(1)} copy(f32[8,72,128]{2,1,0:T(8,128)} %finish.1) | data formatting | bytes 589824 | tf_op jit(solution)/shard_map/finish/pallas_call | solution.py:340
  95.6 0.8 copy.17
Async XLA Ops:
  0.0 1.3 %copy-start = (bf16[8,9,64,128]{3,2,1,0:T(8,128)(2,1)S(1)}, bf16[8,9,64,128]{3,2,1,0:T(8,128)(2,1)}, u32[]{:S(2)}) copy-start(bf16[8,9,64,128]{3,2,1,0:T(8,128)(2,1)} %param.12) | copy-start | bytes 3538948
  1.3 4.1 %copy-start.2 = (f32[64,2,2,64,1,1,1]{3,0,1,2,6,5,4:T(8,128)S(1)}, f32[64,2,2,64,1,1,1]{3,0,1,2,6,5,4:T(8,128)}, u32[]{:S(2)}) copy-start(f32[64,2,2,64,1,1,1]{3,0,1,2,6,5,4:T(8,128)} %constant.29) | copy-start | bytes 196612
  10.1 15.6 %all-to-all-start.1 = ((f32[8,144,128]{2,1,0:T(8,128)}), f32[8,144,128]{2,1,0:T(8,128)S(1)}, u32[]{:S(2)}, u32[]{:S(2)}) async-start(f32[8,144,128]{2,1,0:T(8,128)} %reshape.27), calls=%async_computation.1 | async-start | bytes 1179648 | tf_op jit(solution)/shard_map/all_to_all | solution.py:314
  25.7 30.3 %copy-start.1 = (f32[8,144,128]{2,1,0:T(8,128)}, f32[8,144,128]{2,1,0:T(8,128)S(1)}, u32[]{:S(2)}) copy-start(f32[8,144,128]{2,1,0:T(8,128)S(1)} %all-to-all-done.1) | copy-start | bytes 1769476

commit v2 on v1

--- a/solution.py
+++ b/solution.py
@@ -8,6 +8,7 @@
 from jax.experimental import pallas as pl
 from jax.experimental.pallas import tpu as pltpu
 from jax.sharding import PartitionSpec as P
+
 
 HIGHEST = lax.Precision.HIGHEST
 SUBLANES = 8
@@ -120,6 +121,13 @@
     return np.stack([np.stack([cosine, -sine]), np.stack([sine, cosine])])
 
 
+def split_table(table):
+    table = table.astype(np.float32)
+    high = table.astype(jnp.bfloat16)
+    low = (table - high.astype(np.float32)).astype(jnp.bfloat16)
+    return np.concatenate([high, low], axis=-1)
+
+
 @functools.lru_cache(None)
 def tables(num_fer, num_bos, rows_all, cols):
     devices = num_fer * num_bos
@@ -140,11 +148,16 @@
     ) / rows_all
     t = turn(ky, ry, cols, 1.0) / cols
     to_ky = t.transpose(3, 1, 0, 2).reshape(2 * cols, 2 * cols)
+    places = LANES // (2 * near * num_bos)
     t = turn(ry, ky, cols, 1.0).reshape(2, 2, num_fer, num_bos, near, cols) / cols
-    weight_ry = t.transpose(2, 1, 5, 3, 4, 0).reshape(num_fer, 2 * cols, num_bos * near * 2)
-    weight_rx = turn(rx, kx, rows_all, 1.0).transpose(3, 1, 0, 2) / rows_all
-    out = (to_ry, to_rx, to_kx, to_ky, weight_ry, weight_rx)
-    return tuple(np.ascontiguousarray(x, dtype=np.float32) for x in out)
+    t = np.einsum("oifbnk,pq->fpikonqb", t, np.eye(places))
+    weight_ry = split_table(t.reshape(num_fer, places, 2 * cols, LANES))
+    t = turn(rx, kx, rows_all, 1.0) / rows_all
+    weight_rx = np.einsum("oirk,nm->inkomr", t, eye).reshape(
+        2 * near * rows_all, 2 * near * rows_all
+    )
+    out = (to_ry, to_rx, to_kx, to_ky, weight_rx)
+    return tuple(np.ascontiguousarray(x, dtype=np.float32) for x in out) + (weight_ry,)
 
 
 def nt_dot(a, b):
@@ -195,13 +208,41 @@
         out_ref[pl.ds(row, held), at : at + tile.shape[1]] = tile
 
 
+def send_weight_kernel(num_bos, weight_ref, to_ry_ref, to_rx_ref, *refs):
+    outs, rows_ref = refs[:num_bos], refs[num_bos]
+    groups, places, rows_all, width = weight_ref.shape
+    fer, me = lax.axis_index("fer"), lax.axis_index("bos")
+    both = 0.0
+    for place in range(places):
+        block = weight_ref[:, place].reshape(groups * rows_all, width)
+        both = both + jnp.dot(block, to_ry_ref[fer, place], preferred_element_type=jnp.float32)
+    part = both[:, :LANES] + both[:, LANES:]
+    turned = []
+    deep = places * num_bos
+    for group in range(groups):
+        block = part[group * rows_all : (group + 1) * rows_all].T
+        turned.append(
+            jnp.concatenate([block[i * deep : (i + 1) * deep] for i in range(LANES // deep)], axis=1)
+        )
+    done = nn_dot(jnp.concatenate(turned, axis=0), to_rx_ref[...])
+    size = groups * places * 2
+    for item in range(groups * places):
+        for part in range(2):
+            rows_ref[pl.ds(item * 2 + part, num_bos, stride=size), :] = done[
+                item * num_bos : (item + 1) * num_bos, part * LANES : (part + 1) * LANES
+            ]
+    for hop in range(num_bos):
+        outs[hop][...] = rows_ref[pl.ds(pl.multiple_of((me ^ hop) * size, SUBLANES), size), :]
+
+
 def convolve_kernel(
-    num_fer, num_bos, spans, window, start_ref, order_ref, green_ref, weight_ref, to_rx_ref, to_kx_ref,
-    out_ref, planes_ref, factor_ref, scale_ref,
+    num_fer, num_bos, spans, window, start_ref, order_ref, green_ref, to_rx_ref, to_kx_ref, *refs
 ):
+    weights, (out_ref, planes_ref, factor_ref, scale_ref) = refs[:num_bos], refs[num_bos:]
     held = window // num_fer
     pairs = 9
-    bos_dev = weight_ref.shape[0] // (num_bos * 2 * pairs)
+    bos_dev = weights[0].shape[0] // (2 * pairs)
+    me = lax.axis_index("bos")
     used = spans * pairs * held
     points = LANES
     quads, halves, kx_dev, _ = green_ref.shape
@@ -229,12 +270,14 @@
             planes_ref[pair, where, :] = both[0] + both[1]
             planes_ref[pairs + pair, where, :] = both[0]
             planes_ref[2 * pairs + pair, where, :] = both[1]
-    for cb in range(pairs):
-        re = weight_ref[pl.ds(2 * cb, num_bos * bos_dev, stride=2 * pairs), :]
-        im = weight_ref[pl.ds(2 * cb + 1, num_bos * bos_dev, stride=2 * pairs), :]
-        factor_ref[cb] = re
-        factor_ref[pairs + cb] = im - re
-        factor_ref[2 * pairs + cb] = re + im
+    for hop in range(num_bos):
+        where = pl.ds(hop * bos_dev, bos_dev)
+        for cb in range(pairs):
+            re = weights[hop][pl.ds(2 * cb, bos_dev, stride=2 * pairs), :]
+            im = weights[hop][pl.ds(2 * cb + 1, bos_dev, stride=2 * pairs), :]
+            factor_ref[cb, where, :] = re
+            factor_ref[pairs + cb, where, :] = im - re
+            factor_ref[2 * pairs + cb, where, :] = re + im
     at = used - (halves - 1) * LANES
     for fer in range(num_fer):
         for bos in range(num_bos):
@@ -247,9 +290,10 @@
     for fer in range(num_fer):
 
         def step(p, sums):
-            omega = order_ref[p // bos_dev] * bos_dev + p % bos_dev
+            source = me ^ (p // bos_dev)
+            omega = order_ref[source] * bos_dev + p % bos_dev
             where = pl.ds(fer * held + omega, held)
-            scale = scale_ref[fer * num_bos * bos_dev + p]
+            scale = scale_ref[(fer * num_bos + source) * bos_dev + p % bos_dev]
             sums = list(sums)
             for third in range(3):
                 g = [planes_ref[third * pairs + pair, where, :] for pair in range(pairs)]
@@ -272,26 +316,26 @@
 
 
 def finish_kernel(held, sum_ref, table_ref, out_ref):
-    kx_dev, rows, width = out_ref.shape
-    pairs = rows // held
+    kx_dev, pairs, _, _ = out_ref.shape
+    rows = pairs * held
     deep = sum_ref.shape[0] // kx_dev
     for kx in range(kx_dev):
         block = sum_ref[pl.ds(kx, deep, stride=kx_dev), :]
         done = nn_dot(block.T[:rows], table_ref[...])
         for pair in range(pairs):
-            out_ref[kx, pl.ds(pair, held, stride=pairs), :] = done[pair * held : (pair + 1) * held]
+            out_ref[kx, pair] = done[pair * held : (pair + 1) * held]
 
 
 def real_space_body(green, bos_weight, vertex, block_order, window_start):
     num_fer, num_bos = lax.axis_size("fer"), lax.axis_size("bos")
     devices = num_fer * num_bos
-    num_slot, held, pairs, kx_dev, width = green.shape
+    _, held, pairs, kx_dev, width = green.shape
     bos_dev, _, rows_all, _ = bos_weight.shape
     cols = width // 2
     near = cols // devices
     window = held * num_fer
     spans = -(-(window + num_bos * bos_dev) // window)
-    to_ry, to_rx, to_kx, to_ky, weight_ry, weight_rx = tables(num_fer, num_bos, rows_all, cols)
+    to_ry, to_rx, to_kx, to_ky, weight_rx, weight_ry = tables(num_fer, num_bos, rows_all, cols)
     vmem = pl.BlockSpec(memory_space=pltpu.VMEM)
     smem = pl.BlockSpec(memory_space=pltpu.SMEM)
     lanes = 2 * LANES
@@ -306,19 +350,29 @@
         ],
         name="send_green",
     )(window_start, green, vertex, to_ry)
-    mine = lax.dynamic_index_in_dim(weight_ry, lax.axis_index("fer"), 0, keepdims=False)
-    part = jnp.einsum("pmkc,cd->pmkd", bos_weight.astype(jnp.float32), mine, precision=HIGHEST)
-    part = part.reshape(bos_dev, pairs, rows_all, num_bos, near, 2)
-    factors = jnp.einsum("pmkbni,kior->bpmonr", part, weight_rx, precision=HIGHEST)
-    factors = factors.reshape(num_bos, bos_dev * pairs * 2, near * rows_all)
-    factors = lax.all_to_all(factors, "bos", 0, 0, tiled=True)
     message = message.reshape(devices, 2 * near * 2 * kx_dev, LANES)
+    message, bos_weight = lax.optimization_barrier((message, bos_weight))
     message = lax.all_to_all(message, ("fer", "bos"), 0, 0, tiled=True)
+    places = weight_ry.shape[1]
+    factors = pl.pallas_call(
+        functools.partial(send_weight_kernel, num_bos),
+        out_shape=[jax.ShapeDtypeStruct((bos_dev * pairs * 2, LANES), jnp.float32)] * num_bos,
+        in_specs=[vmem] * 3,
+        out_specs=[vmem] * num_bos,
+        scratch_shapes=[pltpu.VMEM((num_bos * bos_dev * pairs * 2, LANES), jnp.float32)],
+        cost_estimate=pl.CostEstimate(flops=2 * 10**9, bytes_accessed=3 * 10**6, transcendentals=0),
+        name="send_weight",
+    )(bos_weight.reshape(bos_dev * pairs // places, places, rows_all, width), weight_ry, weight_rx)
+    moved = [factors[0]]
+    for hop in range(1, num_bos):
+        moved.append(
+            lax.ppermute(factors[hop], "bos", [(i, i ^ hop) for i in range(num_bos)])
+        )
     total_rows = devices * 2 * near * kx_dev
     sums = pl.pallas_call(
         functools.partial(convolve_kernel, num_fer, num_bos, spans, window),
         out_shape=jax.ShapeDtypeStruct((total_rows, LANES), jnp.float32),
-        in_specs=[smem, smem, vmem, vmem, vmem, vmem],
+        in_specs=[smem, smem] + [vmem] * (3 + num_bos),
         out_specs=vmem,
         scratch_shapes=[
             pltpu.VMEM((3 * pairs, spans * window, LANES), jnp.float32),
@@ -330,26 +384,26 @@
         window_start,
         block_order,
         message.reshape(devices * 2 * near, 2, kx_dev, LANES),
-        factors.reshape(num_bos * bos_dev * pairs * 2, LANES),
         to_rx,
         to_kx,
+        *moved,
     )
     sums = lax.all_to_all(
         sums.reshape(devices, 2 * near * kx_dev, LANES), ("fer", "bos"), 0, 0, tiled=True
     )
     out = pl.pallas_call(
         functools.partial(finish_kernel, held),
-        out_shape=jax.ShapeDtypeStruct((kx_dev, held * pairs, width), jnp.float32),
+        out_shape=jax.ShapeDtypeStruct((kx_dev, pairs, held, width), jnp.float32),
         in_specs=[vmem, vmem],
         out_specs=vmem,
         name="finish",
     )(sums.reshape(total_rows, LANES), to_ky)
-    return out.reshape(kx_dev, held, pairs, width)
+    return out.transpose(0, 2, 1, 3)
 
 
 def body(green, bos_weight, vertex, block_order, window_start):
     devices = lax.axis_size("fer") * lax.axis_size("bos")
-    num_slot, held, pairs, kx_dev, width = green.shape
+    _, held, pairs, kx_dev, width = green.shape
     bos_dev, _, rows_all, _ = bos_weight.shape
     cols = width // 2
     fits = (
@@ -359,9 +413,11 @@
         and width == LANES
         and pairs == 9
         and held == kx_dev == bos_dev == SUBLANES
-    )
-    plan = real_space_body if fits else gathered_body
-    return plan(green, bos_weight, vertex, block_order, window_start)
+        and lax.axis_size("bos") & (lax.axis_size("bos") - 1) == 0
+    )
+    if not fits:
+        return gathered_body(green, bos_weight, vertex, block_order, window_start)
+    return real_space_body(green, bos_weight, vertex, block_order, window_start)
 
 
 def solution(mesh):

time: 96.9 us -> 78.6 us (0.81)
  blocking collectives: 49.6 us -> 19.3 us
  waiting for transfers between devices: 5.6 us -> 14.7 us
  starting transfers between devices: 5.2 us -> 13.6 us
  matrix products: 6.24 us -> 0 us
  Pallas kernels: 23.3 us -> 28.9 us
  local copies, waits for them, and re-layouts: 5.64 us -> 0.96 us
    all_to_all x1 -> x0, blocking collectives: 30.3 us -> none  [real_space_body(): message = lax.all_to_all(message, ('fer', 'bos'), 0, 0, tiled=True)]
    ppermute x0 -> x7, waiting for transfers between devices: none -> 8.97 us  [real_space_body(): lax.ppermute(factors[hop], 'bos', [(i, i ^ hop) for i in range(num_bos)])]
    ppermute x0 -> x7, starting transfers between devices: none -> 6.28 us  [real_space_body(): lax.ppermute(factors[hop], 'bos', [(i, i ^ hop) for i in range(num_bos)])]
    dot_general x2 -> x0, matrix products: 6.24 us -> none  [the longest x1 4.04 us: real_space_body(): jnp.einsum('pmkc,cd->pmkd', bos_weight.astype(jnp.float32), mine, precisi...]
    pallas_call x0 -> x1, Pallas kernels: none -> 5.16 us  [real_space_body(): pl.pallas_call(functools.partial(send_weight_kernel, num_bos), out_shape=...]
    reshape x2 -> x0, local copies, waits for them, and re-layouts: 2.27 us -> none  [the longest x1 1.5 us: real_space_body(): factors = factors.reshape(num_bos, bos_dev * pairs * 2, near * rows_all)]
    all_to_all x1, starting transfers between devices: 5.2 us -> 7.32 us  [real_space_body(): message = lax.all_to_all(message, ('fer', 'bos'), 0, 0, tiled=True)]
    transpose x1 -> x0, local copies, waits for them, and re-layouts: 1.08 us -> none  [real_space_body(): jnp.einsum('pmkbni,kior->bpmonr', part, weight_rx, precision=HIGHEST)]
  transfers between devices with their start and end apart: 1 -> 8, of which waited for: 1 -> 4; matrix products, arithmetic and copies ran while one was open for 0% -> 0% of each run, Pallas kernels for 4% -> 7%
where the time goes in v2:
time: 78.6 us; the launch traced here: 78.3 us
  Pallas kernels  28.9 us (37%)
  blocking collectives  19.3 us (25%)
  waiting for transfers between devices  14.7 us (19%)
  starting transfers between devices  13.6 us (17%)
  local copies, waits for them, and re-layouts  0.96 us (1%)
    all_to_all x1, blocking collectives, real_space_body(): lax.all_to_all(sums.reshape(devices, 2 * near * kx_dev, LANES), ('fer', '...  19.3 us
    pallas_call x1, Pallas kernels, real_space_body(): pl.pallas_call(functools.partial(convolve_kernel, num_fer, num_bos, spans...  17.1 us
    ppermute x7, waiting for transfers between devices, real_space_body(): lax.ppermute(factors[hop], 'bos', [(i, i ^ hop) for i in range(num_bos)])  8.97 us
    all_to_all x1, starting transfers between devices, real_space_body(): message = lax.all_to_all(message, ('fer', 'bos'), 0, 0, tiled=True)  7.32 us
    ppermute x7, starting transfers between devices, real_space_body(): lax.ppermute(factors[hop], 'bos', [(i, i ^ hop) for i in range(num_bos)])  6.28 us
    all_to_all x1, waiting for transfers between devices, real_space_body(): message = lax.all_to_all(message, ('fer', 'bos'), 0, 0, tiled=True)  5.77 us
    pallas_call x1, Pallas kernels, real_space_body(): pl.pallas_call(functools.partial(send_weight_kernel, num_bos), out_shape=...  5.16 us
    pallas_call x1, Pallas kernels, real_space_body(): pl.pallas_call(functools.partial(send_green_kernel, devices, spans, windo...  4.18 us
  transfers between devices with their start and end apart: 8, of which 4 were waited for; matrix products, arithmetic and copies ran while one was open for 0% of the time, Pallas kernels for 7%

profile of v2, /device:TPU:0, one launch (start us, length us, event | category | flops | bytes accessed | tf_op | source)
XLA Modules:
  0.0 78.3 jit_solution(14251048127908138531)
XLA Ops:
  0.7 4.2 %send_green.1 = f32[2048,128]{1,0:T(8,128)} custom-call(s32[1]{0:T(128)S(6)} %copy.12.start_ref, bf16[4,8,9,8,128]{4,3,2,1,0:T(8,128)(2,1)} %green_ref.1, f32[8,8]{1,0:T(8,128)} %vertex_ref.1, f32[128,128]{1,0:T(8,128)} %constant.12.clone.table_ref), custom_call_target="tpu_custom_call" | custom-call | tf_op jit(solution)/shard_map/send_green/pallas_call | solution.py:342
  4.8 7.3 %all-to-all-start = ((f32[32,64,128]{2,1,0:T(8,128)}), f32[32,64,128]{2,1,0:T(8,128)S(1)}, u32[]{:S(2)}, u32[]{:S(2)}) async-start(f32[32,64,128]{2,1,0:T(8,128)} %bitcast.7), calls=%async_computation | async-start | bytes 2097152 | tf_op jit(solution)/shard_map/all_to_all | solution.py:355
  12.2 5.2 %send_weight.1 = (f32[144,128]{1,0:T(8,128)}, f32[144,128]{1,0:T(8,128)}, f32[144,128]{1,0:T(8,128)}, f32[144,128]{1,0:T(8,128)}, f32[144,128]{1,0:T(8,128)}, /*...) custom-call(bf16[18,4,64,128]{3,2,1,0:T(8,128)(2,1)} %bitcast.10, ...), custom_call_target="tpu_custom_call" | custom-call | flops 2000000000 | bytes 3000000 | tf_op jit(solution)/shard_map/send_weight/pallas_call | solution.py:357
  17.3 0.2 collective-permute-start
  17.6 1.6 %collective-permute-start.1 = (f32[144,128]{1,0:T(8,128)}, f32[144,128]{1,0:T(8,128)S(1)}, u32[]{:S(2)}, u32[]{:S(2)}) collective-permute-start(f32[144,128]{1,0:T(8,128)} %get-tuple-element.19), channel_id=1, source_target_pairs={{0,2},{1,3},{2,0},{3,1},{4,6},{5,7},{6,4},{7,5},{8,10},{9,11},{10,... | collective-permute-start | bytes 221192 | tf_op jit(solution)/shard_map/ppermute | solution.py:369
  19.2 0.0 collective-permute-start.2
  19.2 1.7 %collective-permute-start.3 = (f32[144,128]{1,0:T(8,128)}, f32[144,128]{1,0:T(8,128)S(1)}, u32[]{:S(2)}, u32[]{:S(2)}) collective-permute-start(f32[144,128]{1,0:T(8,128)} %get-tuple-element.21), channel_id=1, source_target_pairs={{0,4},{1,5},{2,6},{3,7},{4,0},{5,1},{6,2},{7,3},{8,12},{9,13},{10,... | collective-permute-start | bytes 221192 | tf_op jit(solution)/shard_map/ppermute | solution.py:369
  21.0 0.1 collective-permute-start.4
  21.1 0.0 collective-permute-done.refs_1_
  21.1 0.0 copy-start.1
  21.1 2.5 %collective-permute-start.5 = (f32[144,128]{1,0:T(8,128)}, f32[144,128]{1,0:T(8,128)S(1)}, u32[]{:S(2)}, u32[]{:S(2)}) collective-permute-start(f32[144,128]{1,0:T(8,128)} %get-tuple-element.23), channel_id=1, source_target_pairs={{0,6},{1,7},{2,4},{3,5},{4,2},{5,3},{6,0},{7,1},{8,14},{9,15},{10,... | collective-permute-start | bytes 221192 | tf_op jit(solution)/shard_map/ppermute | solution.py:369
  23.6 1.2 %collective-permute-done.1.refs_2_ = f32[144,128]{1,0:T(8,128)S(1)} collective-permute-done((f32[144,128]{1,0:T(8,128)}, f32[144,128]{1,0:T(8,128)S(1)}, u32[]{:S(2)}, u32[]{:S(2)}) %collective-permute-start.1) | collective-permute-done | bytes 73760 | tf_op jit(solution)/shard_map/ppermute | solution.py:369
  24.8 0.0 copy-start.2
  24.8 0.0 collective-permute-start.6
  24.8 2.4 %collective-permute-done.2.refs_3_ = f32[144,128]{1,0:T(8,128)S(1)} collective-permute-done((f32[144,128]{1,0:T(8,128)}, f32[144,128]{1,0:T(8,128)S(1)}, u32[]{:S(2)}, u32[]{:S(2)}) %collective-permute-start.2) | collective-permute-done | bytes 73760 | tf_op jit(solution)/shard_map/ppermute | solution.py:369
  27.1 0.0 collective-permute-done.3.refs_4_
  27.2 5.4 %collective-permute-done.4.refs_5_ = f32[144,128]{1,0:T(8,128)S(1)} collective-permute-done((f32[144,128]{1,0:T(8,128)}, f32[144,128]{1,0:T(8,128)S(1)}, u32[]{:S(2)}, u32[]{:S(2)}) %collective-permute-start.4) | collective-permute-done | bytes 73760 | tf_op jit(solution)/shard_map/ppermute | solution.py:369
  32.6 0.0 collective-permute-done.5.refs_6_
  32.6 0.0 collective-permute-done.6.refs_7_
  32.6 0.0 copy-start.7
  32.6 5.8 %all-to-all-done = f32[32,64,128]{2,1,0:T(8,128)S(1)} async-done(((f32[32,64,128]{2,1,0:T(8,128)}), f32[32,64,128]{2,1,0:T(8,128)S(1)}, u32[]{:S(2)}, u32[]{:S(2)}) %all-to-all-start) | async-done | bytes 1048608 | tf_op jit(solution)/shard_map/all_to_all | solution.py:355
  38.4 0.0 copy-done.1
  38.4 0.0 copy-done.2
  38.4 0.0 copy-done.3
  38.4 0.0 copy-done.4
  38.4 0.0 copy-done.5
  38.4 0.0 copy-done.6
  38.4 0.0 copy-done.7
  38.4 0.9 %copy-done = f32[32,64,128]{2,1,0:T(8,128)} copy-done((f32[32,64,128]{2,1,0:T(8,128)}, f32[32,64,128]{2,1,0:T(8,128)S(1)}, u32[]{:S(2)}) %copy-start) | copy-done | bytes 1048600
  39.4 17.1 %convolve.1 = f32[1024,128]{1,0:T(8,128)} custom-call(s32[1]{0:T(128)S(6)} %copy.12.start_ref, s32[8]{0:T(128)} %order_ref.1, f32[128,2,8,128]{3,2,1,0:T(8,128)} %bitcast.6, f32[256,256]{1,0:T(8,128)} %constant.15.clone.to_rx_ref, f32[256,256]{1,0:T(8,128)} %constant.16.clone.to_kx_ref, f32[144,128]{1,0:T(8,128)} %get-tuple-element.17.refs_0_, ...), custom_call_target="tpu_custom_call" | custom-call | tf_op jit(solution)/shard_map/convolve/pallas_call | solution.py:372
  56.5 19.3 %all_to_all.10 = f32[32,32,128]{2,1,0:T(8,128)} all-to-all(f32[32,32,128]{2,1,0:T(8,128)} %bitcast.8), channel_id=1, replica_groups=mesh['fer'=4,'bos'=8] {'fer','bos'}, dimensions={0} | all-to-all | bytes 1048576 | tf_op jit(solution)/shard_map/all_to_all | solution.py:391
  75.8 2.4 %finish.1 = f32[8,9,8,128]{3,2,1,0:T(8,128)} custom-call(f32[1024,128]{1,0:T(8,128)} %bitcast.9, f32[128,128]{1,0:T(8,128)} %constant.17.clone.table_ref), custom_call_target="tpu_custom_call" | custom-call | tf_op jit(solution)/shard_map/finish/pallas_call | solution.py:394
  (5 shorter events, 0.0 us)
Async XLA Ops:
  4.8 33.5 %all-to-all-start = ((f32[32,64,128]{2,1,0:T(8,128)}), f32[32,64,128]{2,1,0:T(8,128)S(1)}, u32[]{:S(2)}, u32[]{:S(2)}) async-start(f32[32,64,128]{2,1,0:T(8,128)} %bitcast.7), calls=%async_computation | async-start | bytes 2097152 | tf_op jit(solution)/shard_map/all_to_all | solution.py:355
  17.3 3.7 %collective-permute-start = (f32[144,128]{1,0:T(8,128)}, f32[144,128]{1,0:T(8,128)S(1)}, u32[]{:S(2)}, u32[]{:S(2)}) collective-permute-start(f32[144,128]{1,0:T(8,128)} %get-tuple-element.18), channel_id=1, source_target_pairs={{0,1},{1,0},{2,3},{3,2},{4,5},{5,4},{6,7},{7,6},{8,9},{9,8},{10,11... | collective-permute-start | bytes 221192 | tf_op jit(solution)/shard_map/ppermute | solution.py:369
  17.6 7.2 %collective-permute-start.1 = (f32[144,128]{1,0:T(8,128)}, f32[144,128]{1,0:T(8,128)S(1)}, u32[]{:S(2)}, u32[]{:S(2)}) collective-permute-start(f32[144,128]{1,0:T(8,128)} %get-tuple-element.19), channel_id=1, source_target_pairs={{0,2},{1,3},{2,0},{3,1},{4,6},{5,7},{6,4},{7,5},{8,10},{9,11},{10,... | collective-permute-start | bytes 221192 | tf_op jit(solution)/shard_map/ppermute | solution.py:369
  19.2 7.9 %collective-permute-start.2 = (f32[144,128]{1,0:T(8,128)}, f32[144,128]{1,0:T(8,128)S(1)}, u32[]{:S(2)}, u32[]{:S(2)}) collective-permute-start(f32[144,128]{1,0:T(8,128)} %get-tuple-element.20), channel_id=1, source_target_pairs={{0,3},{1,2},{2,1},{3,0},{4,7},{5,6},{6,5},{7,4},{8,11},{9,10},{10,... | collective-permute-start | bytes 221192 | tf_op jit(solution)/shard_map/ppermute | solution.py:369
  19.2 7.9 %collective-permute-start.3 = (f32[144,128]{1,0:T(8,128)}, f32[144,128]{1,0:T(8,128)S(1)}, u32[]{:S(2)}, u32[]{:S(2)}) collective-permute-start(f32[144,128]{1,0:T(8,128)} %get-tuple-element.21), channel_id=1, source_target_pairs={{0,4},{1,5},{2,6},{3,7},{4,0},{5,1},{6,2},{7,3},{8,12},{9,13},{10,... | collective-permute-start | bytes 221192 | tf_op jit(solution)/shard_map/ppermute | solution.py:369
  21.0 11.6 %collective-permute-start.4 = (f32[144,128]{1,0:T(8,128)}, f32[144,128]{1,0:T(8,128)S(1)}, u32[]{:S(2)}, u32[]{:S(2)}) collective-permute-start(f32[144,128]{1,0:T(8,128)} %get-tuple-element.22), channel_id=1, source_target_pairs={{0,5},{1,4},{2,7},{3,6},{4,1},{5,0},{6,3},{7,2},{8,13},{9,12},{10,... | collective-permute-start | bytes 221192 | tf_op jit(solution)/shard_map/ppermute | solution.py:369
  21.1 17.3 %copy-start.1 = (f32[144,128]{1,0:T(8,128)}, f32[144,128]{1,0:T(8,128)S(1)}, u32[]{:S(2)}) copy-start(f32[144,128]{1,0:T(8,128)S(1)} %collective-permute-done.refs_1_) | copy-start | bytes 221188
  21.1 11.5 %collective-permute-start.5 = (f32[144,128]{1,0:T(8,128)}, f32[144,128]{1,0:T(8,128)S(1)}, u32[]{:S(2)}, u32[]{:S(2)}) collective-permute-start(f32[144,128]{1,0:T(8,128)} %get-tuple-element.23), channel_id=1, source_target_pairs={{0,6},{1,7},{2,4},{3,5},{4,2},{5,3},{6,0},{7,1},{8,14},{9,15},{10,... | collective-permute-start | bytes 221192 | tf_op jit(solution)/shard_map/ppermute | solution.py:369
  24.8 13.6 %copy-start.2 = (f32[144,128]{1,0:T(8,128)}, f32[144,128]{1,0:T(8,128)S(1)}, u32[]{:S(2)}) copy-start(f32[144,128]{1,0:T(8,128)S(1)} %collective-permute-done.1.refs_2_) | copy-start | bytes 221188
  24.8 7.8 %collective-permute-start.6 = (f32[144,128]{1,0:T(8,128)}, f32[144,128]{1,0:T(8,128)S(1)}, u32[]{:S(2)}, u32[]{:S(2)}) collective-permute-start(f32[144,128]{1,0:T(8,128)} %get-tuple-element.24), channel_id=1, source_target_pairs={{0,7},{1,6},{2,5},{3,4},{4,3},{5,2},{6,1},{7,0},{8,15},{9,14},{10,... | collective-permute-start | bytes 221192 | tf_op jit(solution)/shard_map/ppermute | solution.py:369
  27.1 11.2 %copy-start.3 = (f32[144,128]{1,0:T(8,128)}, f32[144,128]{1,0:T(8,128)S(1)}, u32[]{:S(2)}) copy-start(f32[144,128]{1,0:T(8,128)S(1)} %collective-permute-done.2.refs_3_) | copy-start | bytes 221188
  27.2 11.2 %copy-start.4 = (f32[144,128]{1,0:T(8,128)}, f32[144,128]{1,0:T(8,128)S(1)}, u32[]{:S(2)}) copy-start(f32[144,128]{1,0:T(8,128)S(1)} %collective-permute-done.3.refs_4_) | copy-start | bytes 221188
  32.6 5.8 %copy-start.5 = (f32[144,128]{1,0:T(8,128)}, f32[144,128]{1,0:T(8,128)S(1)}, u32[]{:S(2)}) copy-start(f32[144,128]{1,0:T(8,128)S(1)} %collective-permute-done.4.refs_5_) | copy-start | bytes 221188
  32.6 5.8 %copy-start.6 = (f32[144,128]{1,0:T(8,128)}, f32[144,128]{1,0:T(8,128)S(1)}, u32[]{:S(2)}) copy-start(f32[144,128]{1,0:T(8,128)S(1)} %collective-permute-done.5.refs_6_) | copy-start | bytes 221188
  32.6 5.8 %copy-start.7 = (f32[144,128]{1,0:T(8,128)}, f32[144,128]{1,0:T(8,128)S(1)}, u32[]{:S(2)}) copy-start(f32[144,128]{1,0:T(8,128)S(1)} %collective-permute-done.6.refs_7_) | copy-start | bytes 221188
  38.4 1.0 %copy-start = (f32[32,64,128]{2,1,0:T(8,128)}, f32[32,64,128]{2,1,0:T(8,128)S(1)}, u32[]{:S(2)}) copy-start(f32[32,64,128]{2,1,0:T(8,128)S(1)} %all-to-all-done) | copy-start | bytes 3145732
